TPU v7x, 256 devices: a whole 4x4x8 slice. The times are simulated.
256 devices in a mesh: ctx: 8 (over x, y_hi), mp: 32 (over z, y_lo, core).
Axes of the slice: x: 4, y: 4 (y_hi: 2, y_lo: 2; y = y_hi * 2 + y_lo), z: 8, core: 2. Of those that a mesh axis runs over, the one named last changes fastest.
Arguments:
- activations: bfloat16 [8192, 4096], P('ctx', 'mp'), may hold values from -36 to 36
- norm_gain: float32 [4096], P('mp'), may hold values from 0.1 to 1.9
- w_in: bfloat16 [4096, 3, 4096], P('ctx', None, 'mp'), may hold values from -0.09375 to 0.09375
- tail_rows: bfloat16 [3, 4096, 2], P(None, 'mp'), may hold values from -4 to 4
- short_filter: float32 [3, 3, 4096], P(None, None, 'mp'), may hold values from -3 to 3
- decay_rate: float32 [4096, 16], P('mp'), may hold values from 2.4414063e-05 to 0.08, as said below
- residue: float32 [4096, 16], P('mp'), may hold values from -1.5 to 1.5
- skip_gain: float32 [4096], P('mp'), may hold values from -4 to 4
- state_in: float32 [4096, 16], P('mp'), may hold values from -4 to 4
- w_out: bfloat16 [4096, 4096], P('mp', 'ctx'), may hold values from -0.1875 to 0.1875
Outputs:
- block_out: bfloat16 [8192, 4096], P('ctx', 'mp')
- state_out: float32 [4096, 16], P('mp')
Inputs may be any that keep to these rules, and one draw needn't show every extreme that they name: `decay_rate`: every rate lies between 0.2/8192 and 0.08; any share of the modes may be slow (below 2/8192) or fast.
All inputs are finite; a program needn't handle non-finite values.
Results may differ from a plain program's by a relative error of at most 0.03.
Values may be sent and summed in bfloat16 or wider, within the bound.
A program may use at most 64 MiB of HBM per device.

v0:
```python
import math
import jax
import jax.numpy as jnp
import numpy as np
from jax import lax
from jax.sharding import PartitionSpec as P

highest = lax.Precision.HIGHEST


def from_behind(block, axis, distance):
    devices = range(lax.axis_size(axis))
    route = [(i - distance, i) for i in devices if i - distance in devices]
    return lax.ppermute(block, axis, route)


def pick_rows(array_in, offset, share):
    return lax.dynamic_slice_in_dim(array_in, offset, share, 0)


def chain_step(first, second):
    return (first[0] * second[0], second[0] * first[1] + second[1])


def block_powers(rate_rows, block_size):
    steps_in = jnp.arange(block_size, dtype=jnp.float32)
    return jnp.exp(-rate_rows[:, :, None] * steps_in[None, None, :])


def carried_response(entering, rate_rows, residues, block_size):
    powers = block_powers(rate_rows, block_size)
    lifted = residues[:, :, None] * jnp.exp(-rate_rows)[:, :, None] * powers
    return jnp.einsum("ckn,cnt->ckt", entering, lifted, precision=highest)


def initial_response(initial, rate_rows, residues, length):
    block_size = math.gcd(64, length)
    blocks = length // block_size
    index_k = jnp.arange(blocks, dtype=jnp.float32) * block_size
    carried = jnp.exp(-rate_rows[:, None, :] * index_k[None, :, None]) * initial[:, None, :]
    return carried_response(carried, rate_rows, residues, block_size).reshape(
        initial.shape[0], length
    )


def modal_conv(signal, rate_rows, residues, skip_rows, initial):
    channels, length = signal.shape
    block_size = math.gcd(64, length)
    blocks = length // block_size
    values = signal.astype(jnp.float32)
    shaped = values.reshape(channels, blocks, block_size)
    powers = block_powers(rate_rows, block_size)
    scales = jnp.sqrt(-jnp.expm1(-2.0 * rate_rows))
    kernel = jnp.einsum("cn,cnb->cb", residues * scales, powers, precision=highest)
    offsets = np.arange(block_size)[:, None] - np.arange(block_size)[None, :]
    clipped = np.clip(offsets, 0, block_size - 1)
    toeplitz = jnp.where(offsets[None] >= 0, kernel[:, clipped], 0.0)
    within = jnp.einsum("cts,cks->ckt", toeplitz, shaped, precision=highest)
    loading = jnp.einsum(
        "cks,cns->ckn", shaped, scales[:, :, None] * powers[:, :, ::-1], precision=highest
    )
    decays = jnp.broadcast_to(jnp.exp(-rate_rows * block_size)[:, None, :], loading.shape)
    decay_all, block_ends = lax.associative_scan(chain_step, (decays, loading), axis=1)
    entering = jnp.concatenate([jnp.zeros_like(block_ends[:, :1]), block_ends[:, :-1]], axis=1)
    response = (within + carried_response(entering, rate_rows, residues, block_size)).reshape(
        channels, length
    )
    response = response + initial_response(initial, rate_rows, residues, length)
    final = block_ends[:, -1] + jnp.exp(-rate_rows * length) * initial
    return (response + skip_rows[:, None] * values, final)


def local(
    activations,
    norm_gain,
    w_in,
    tail_rows,
    short_filter,
    decay_rate,
    residue,
    skip_gain,
    state_in,
    w_out,
):
    tok_rows, feature_width = activations.shape
    model_width = feature_width * lax.axis_size("mp")
    act_float = activations.astype(jnp.float32)
    squares = lax.psum(jnp.sum(act_float * act_float, axis=1), "mp")
    inverse = lax.rsqrt(squares / model_width + 1e-06)
    normed = (act_float * inverse[:, None] * norm_gain[None, :]).astype(jnp.bfloat16)
    panel = lax.all_gather(w_in, "ctx", axis=0, tiled=True).reshape(model_width, 3 * feature_width)
    proj_sum = lax.dot_general(
        panel,
        lax.all_gather(normed, "mp", axis=1, tiled=True),
        (((0,), (1,)), ((), ())),
        preferred_element_type=jnp.float32,
    )
    projected = proj_sum.astype(jnp.bfloat16).reshape(3, feature_width, tok_rows)
    incoming = from_behind(projected[:, :, -2:], "ctx", 1)
    incoming = jnp.where(lax.axis_index("ctx") == 0, tail_rows, incoming)
    extended = jnp.concatenate([incoming, projected], axis=2).astype(jnp.float32)
    smoothed = short_filter[0][:, :, None] * extended[:, :, 2:]
    smoothed = smoothed + short_filter[1][:, :, None] * extended[:, :, 1:-1]
    smoothed = smoothed + short_filter[2][:, :, None] * extended[:, :, :-2]
    query = smoothed[0]
    mixed = (smoothed[1] * smoothed[2]).astype(jnp.bfloat16)
    share = feature_width // lax.axis_size("ctx")
    offset = lax.axis_index("ctx") * share
    whole = lax.all_to_all(mixed, "ctx", split_axis=0, concat_axis=1, tiled=True)
    filtered, final_part = modal_conv(
        whole,
        pick_rows(decay_rate, offset, share),
        pick_rows(residue, offset, share),
        pick_rows(skip_gain, offset, share),
        pick_rows(state_in, offset, share),
    )
    response = lax.all_to_all(filtered, "ctx", split_axis=1, concat_axis=0, tiled=True)
    final_state = lax.all_gather(final_part, "ctx", axis=0, tiled=True)
    gated = (query * response).astype(jnp.bfloat16)
    out_panel = lax.all_gather(w_out, "ctx", axis=1, tiled=True)
    branch = (
        lax.psum_scatter(
            lax.dot_general(
                out_panel, gated, (((0,), (0,)), ((), ())), preferred_element_type=jnp.float32
            ).astype(jnp.bfloat16),
            "mp",
            scatter_dimension=0,
            tiled=True,
        )
        .astype(jnp.float32)
        .T
    )
    return ((act_float + branch).astype(jnp.bfloat16), final_state)


def solution(mesh):
    placed = (
        P("ctx", "mp"),
        P("mp"),
        P("ctx", None, "mp"),
        P(None, "mp", None),
        P(None, None, "mp"),
        P("mp", None),
        P("mp", None),
        P("mp"),
        P("mp", None),
        P("mp", "ctx"),
    )
    return jax.shard_map(
        local,
        mesh=mesh,
        in_specs=placed,
        out_specs=(P("ctx", "mp"), P("mp", None)),
        check_vma=False,
    )
```

profile of v0, /device:TPU:4, one launch (start us, length us, event | category | flops | bytes accessed | tf_op | source)
XLA Modules:
  0.0 457.9 jit_solution(16043692956074559367)
XLA Ops:
  10.4 59.9 %psum.7 = f32[1024]{0:T(1024)S(1)} all-reduce(f32[1024]{0:T(1024)S(1)} %fusion.2), channel_id=1, replica_groups=mesh['ctx'=8,'mp'=32] {'mp'}, use_global_device_ids=true, to_apply=%region_1.0 | all-reduce | flops 1024 | bytes 8192 | tf_op jit(solution)/shard_map/psum | solution.py:88
  73.9 11.3 %all-gather.6.cloned.1.call-done = bf16[4096,3,128]{0,2,1:T(8,128)(2,1)} async-done(((bf16[512,3,128]{0,2,1:T(8,128)(2,1)}), bf16[4096,3,128]{0,2,1:T(8,128)(2,1)}) %all-gather.6.cloned.1.call-update) | async-done | bytes 3145744 | tf_op jit(solution)/shard_map/all_gather | solution.py:91
  85.3 92.4 %all-gather.4.cloned.1.call-done = bf16[1024,4096]{1,0:T(8,128)(2,1)} async-done(((bf16[1024,128]{1,0:T(8,128)(2,1)}), bf16[1024,4096]{1,0:T(8,128)(2,1)}) %all-gather.4.cloned.1.call-update) | async-done | bytes 8388624 | tf_op jit(solution)/shard_map/all_gather | solution.py:94
  177.6 7.7 %convolution_convert_fusion = bf16[1024,384]{0,1:T(8,128)(2,1)S(1)} fusion(bf16[1024,4096]{1,0:T(8,128)(2,1)} %all-gather.4.cloned.1.call-done, bf16[4096,384]{0,1:T(8,128)(2,1)} %bitcast.65), kind=kOutput, calls=%fused_computation.7 | convolution fusion | flops 3221618688 | bytes 12320768 | tf_op jit(solution)/shard_map/dot_general | solution.py:92
  185.5 3.9 collective-permute-start
  189.7 5.1 %collective-permute-done = bf16[3,128,2]{2,1,0:T(8,128)(2,1)S(1)} collective-permute-done((bf16[3,128,2]{2,1,0:T(8,128)(2,1)S(1)}, bf16[3,128,2]{2,1,0:T(8,128)(2,1)S(1)}, u32[]{:S(2)}, u32[]{:S(2)}) %collective-permute-start) | collective-permute-done | bytes 1568 | tf_op jit(solution)/shard_map/ppermute | solution.py:14
  197.2 6.7 %all-to-all-start = ((bf16[8,16,1024]{2,1,0:T(8,128)(2,1)}), bf16[8,16,1024]{2,1,0:T(8,128)(2,1)S(1)}, u32[]{:S(2)}, u32[]{:S(2)}) async-start(bf16[8,16,1024]{2,1,0:T(8,128)(2,1)} %bitcast.7), calls=%async_computation | async-start | bytes 524288 | tf_op jit(solution)/shard_map/all_to_all | solution.py:109
  207.4 2.8 all-to-all-done
  211.7 2.9 slice.235
  214.6 2.3 slice.195
  217.0 2.3 slice.194
  235.8 6.2 %pad.47 = f32[16,4,16]{1,2,0:T(8,128)S(1)} pad(f32[16,2,16]{1,2,0:T(8,128)} %pad_add_fusion, f32[]{:T(128)} %constant.7.clone.1), padding=0_0_0x1_0_1x0_0_0 | pad | bytes 6148 | tf_op jit(solution)/shard_map/pad | solution.py:63
  256.0 2.1 pad.54
  258.1 2.2 pad.55
  260.3 3.2 pad.95
  263.5 3.2 pad.57
  267.0 3.2 pad.56
  270.9 14.2 %gather_fusion = f32[4096,16]{1,0:T(8,128)} fusion(f32[16,64]{0,1:T(8,128)S(1)} %bitcast.53, s32[4096]{0:T(1024)S(1)} %copy-done.5), kind=kCustom, calls=%fused_computation | custom fusion | bytes 540672 | tf_op jit(solution)/shard_map/gather | solution.py:57
  285.1 2.3 copy.90
  291.9 12.7 %all_to_all.29 = f32[16,8,1024]{2,0,1:T(8,128)S(1)} all-to-all(f32[16,8,1024]{2,0,1:T(8,128)S(1)} %copy_add_fusion), channel_id=1, replica_groups=mesh['ctx'=8,'mp'=32] {'ctx'}, dimensions={1} | all-to-all | bytes 1048576 | tf_op jit(solution)/shard_map/all_to_all | solution.py:117
  304.7 6.9 %convert_bitcast_fusion = bf16[4096,1024]{0,1:T(8,128)(2,1)} fusion(bf16[128,1024]{1,0:T(8,128)(2,1)S(1)} %fusion.8, bf16[128,4096]{1,0:T(8,128)(2,1)} %all-gather.8.cloned.1.call-done), kind=kOutput, calls=%fused_computation.1 | convolution fusion | flops 1077936128 | bytes 9699328 | tf_op jit(solution)/shard_map/dot_general | solution.py:123
  311.6 11.9 %copy.103 = bf16[4096,1024]{1,0:T(8,128)(2,1)} copy(bf16[4096,1024]{0,1:T(8,128)(2,1)} %convert_bitcast_fusion) | data formatting | bytes 16777216
  323.5 32.6 %all_gather.15 = f32[128,16]{1,0:T(8,128)S(1)} all-gather(f32[16,16]{1,0:T(8,128)S(1)} %get-tuple-element.20), channel_id=1, replica_groups=mesh['ctx'=8,'mp'=32] {'ctx'}, dimensions={0}, use_global_device_ids=true | all-gather | bytes 9216 | tf_op jit(solution)/shard_map/all_gather | solution.py:118
  356.8 92.7 %reduce-scatter.4.cloned.1.call-done = bf16[128,1024]{1,0:T(8,128)(2,1)} async-done(((bf16[4096,1024]{1,0:T(8,128)(2,1)}), bf16[128,1024]{1,0:T(8,128)(2,1)}) %reduce-scatter.4.cloned.1.call-update) | async-done | bytes 262160
  (143 shorter events, 52.5 us)
Async XLA Ops:
  7.2 182.2 %copy-start = (f32[128,16]{0,1:T(8,128)S(1)}, f32[128,16]{0,1:T(8,128)}, u32[]{:S(2)}) copy-start(f32[128,16]{0,1:T(8,128)} %param.19) | copy-start | bytes 24580
  7.2 65.8 %copy-start.18 = (f32[3,3,128]{2,1,0:T(4,128)S(1)}, f32[3,3,128]{2,1,0:T(4,128)}, u32[]{:S(2)}) copy-start(f32[3,3,128]{2,1,0:T(4,128)} %param.17) | copy-start | bytes 13828
  7.2 65.8 %copy-start.16 = (f32[128,16]{0,1:T(8,128)S(1)}, f32[128,16]{0,1:T(8,128)}, u32[]{:S(2)}) copy-start(f32[128,16]{0,1:T(8,128)} %param.21) | copy-start | bytes 24580
  7.2 65.8 %copy-start.17 = (f32[128,16]{0,1:T(8,128)S(1)}, f32[128,16]{0,1:T(8,128)}, u32[]{:S(2)}) copy-start(f32[128,16]{0,1:T(8,128)} %param.18) | copy-start | bytes 24580
  7.2 78.0 %all-gather.6.cloned.1.call-start = ((), (), s32[]{:S(2)}) async-start(), calls=%async_computation.4 | async-start | bytes 3538944 | tf_op jit(solution)/shard_map/all_gather | solution.py:91
  9.2 168.4 %all-gather.4.cloned.1.call-start = ((), (), s32[]{:S(2)}) async-start(), calls=%async_computation.3 | async-start | bytes 8650752 | tf_op jit(solution)/shard_map/all_gather | solution.py:94
  72.2 232.5 %all-gather.8.cloned.1.call-start = ((), (), s32[]{:S(2)}) async-start(), calls=%async_computation.5 | async-start | bytes 1179648 | tf_op jit(solution)/shard_map/all_gather | solution.py:120
  73.2 112.2 %copy-start.11 = (f32[16,16]{1,0:T(8,128)}, f32[16,16]{1,0:T(8,128)S(1)}, u32[]{:S(2)}) copy-start(f32[16,16]{1,0:T(8,128)S(1)} %copy.106) | copy-start | bytes 3076
  73.8 145.5 %copy-start.7 = (f32[16,16]{1,0:T(8,128)}, f32[16,16]{1,0:T(8,128)S(1)}, u32[]{:S(2)}) copy-start(f32[16,16]{1,0:T(8,128)S(1)} %get-tuple-element.27) | copy-start | bytes 3076
  73.8 150.0 %copy-start.9 = (f32[16,16]{1,0:T(8,128)}, f32[16,16]{1,0:T(8,128)S(1)}, u32[]{:S(2)}) copy-start(f32[16,16]{1,0:T(8,128)S(1)} %get-tuple-element.28) | copy-start | bytes 3076
  73.8 152.8 %copy-start.10 = (f32[16,16]{1,0:T(8,128)}, f32[16,16]{1,0:T(8,128)S(1)}, u32[]{:S(2)}) copy-start(f32[16,16]{1,0:T(8,128)S(1)} %get-tuple-element.22) | copy-start | bytes 3076
  177.6 11.9 %copy-start.19 = (bf16[3,128,2]{1,2,0:T(2,128)(2,1)S(1)}, bf16[3,128,2]{1,2,0:T(2,128)(2,1)}, u32[]{:S(2)}) copy-start(bf16[3,128,2]{1,2,0:T(2,128)(2,1)} %param.16) | copy-start | bytes 4612
  185.5 9.4 %collective-permute-start = (bf16[3,128,2]{2,1,0:T(8,128)(2,1)S(1)}, bf16[3,128,2]{2,1,0:T(8,128)(2,1)S(1)}, u32[]{:S(2)}, u32[]{:S(2)}) collective-permute-start(bf16[3,128,2]{2,1,0:T(8,128)(2,1)S(1)} %slice.240), channel_id=1, source_target_pairs={{0,32},{32,64},{64,96},{96,128},{128,160},{160,192},{192,224},{1,3... | collective-permute-start | bytes 4616 | tf_op jit(solution)/shard_map/ppermute | solution.py:14
  196.4 10.4 %copy-start.14 = (s32[4096]{0:T(1024)S(1)}, s32[4096]{0:T(1024)}, u32[]{:S(2)}) copy-start(s32[4096]{0:T(1024)} %constant.70) | copy-start | bytes 49156
  197.2 13.0 %all-to-all-start = ((bf16[8,16,1024]{2,1,0:T(8,128)(2,1)}), bf16[8,16,1024]{2,1,0:T(8,128)(2,1)S(1)}, u32[]{:S(2)}, u32[]{:S(2)}) async-start(bf16[8,16,1024]{2,1,0:T(8,128)(2,1)} %bitcast.7), calls=%async_computation | async-start | bytes 524288 | tf_op jit(solution)/shard_map/all_to_all | solution.py:109
  203.9 245.6 %reduce-scatter.4.cloned.1.call-start = ((), (), s32[]{:S(2)}) async-start(), calls=%async_computation.6 | async-start | bytes 8650752
  246.9 8.1 %copy-start.3 = (f32[16,31,16]{1,2,0:T(8,128)S(1)}, f32[16,31,16]{1,2,0:T(8,128)}, u32[]{:S(2)}) copy-start(f32[16,31,16]{1,2,0:T(8,128)} %slice.233) | copy-start | bytes 95236
  251.6 15.1 %copy-start.2 = (f32[16,63,16]{1,2,0:T(8,128)S(1)}, f32[16,63,16]{1,2,0:T(8,128)}, u32[]{:S(2)}) copy-start(f32[16,63,16]{1,2,0:T(8,128)} %slice.235) | copy-start | bytes 193540
  251.6 15.1 %copy-start.8 = (f32[16,16]{1,0:T(8,128)S(1)}, f32[16,16]{1,0:T(8,128)}, u32[]{:S(2)}) copy-start(f32[16,16]{1,0:T(8,128)} %copy-done.7) | copy-start | bytes 3076
  255.8 14.6 %copy-start.6 = (f32[16,16]{1,0:T(8,128)S(1)}, f32[16,16]{1,0:T(8,128)}, u32[]{:S(2)}) copy-start(f32[16,16]{1,0:T(8,128)} %copy.107) | copy-start | bytes 3076
  255.8 14.6 %copy-start.12 = (f32[16,16]{1,0:T(8,128)S(1)}, f32[16,16]{1,0:T(8,128)}, u32[]{:S(2)}) copy-start(f32[16,16]{1,0:T(8,128)} %copy-done.11) | copy-start | bytes 3076
  255.8 14.6 %copy-start.13 = (f32[16,16]{1,0:T(8,128)S(1)}, f32[16,16]{1,0:T(8,128)}, u32[]{:S(2)}) copy-start(f32[16,16]{1,0:T(8,128)} %copy.105) | copy-start | bytes 3076
  256.0 14.9 %copy-start.5 = (s32[4096]{0:T(1024)S(1)}, s32[4096]{0:T(1024)}, u32[]{:S(2)}) copy-start(s32[4096]{0:T(1024)} %broadcast_clamp_fusion) | copy-start | bytes 49156
  323.5 127.2 %copy-start.1 = (bf16[1024,128]{1,0:T(8,128)(2,1)S(1)}, bf16[1024,128]{1,0:T(8,128)(2,1)}, u32[]{:S(2)}) copy-start(bf16[1024,128]{1,0:T(8,128)(2,1)} %param.13) | copy-start | bytes 786436
  (5 other events, 20.8 us)
Sparse Core Ops, SparseCore 0:
  10.5 74.6 all-gather.5
  87.6 89.9 all-gather.3
  180.1 49.9 all-gather.7
  323.6 125.8 reduce-scatter.3
where the time goes:
time: 459 us; the launch traced here: 458 us
  waiting for transfers between devices  205 us (45%)
  blocking collectives  105 us (23%)
  local copies, waits for them, and re-layouts  85.8 us (19%)
  matrix products  19.3 us (4%)
  other arithmetic  17.2 us (4%)
  between operations  14.5 us (3%)
  starting transfers between devices  10.7 us (2%)
    unnamed x5, waiting for transfers between devices  93.4 us
    all_gather x1, waiting for transfers between devices, local(): lax.all_gather(normed, 'mp', axis=1, tiled=True)  92.4 us
    psum x1, blocking collectives, local(): squares = lax.psum(jnp.sum(act_float * act_float, axis=1), 'mp')  59.9 us
    all_gather x1, blocking collectives, local(): final_state = lax.all_gather(final_part, 'ctx', axis=0, tiled=True)  32.6 us
    pad x12, local copies, waits for them, and re-layouts, modal_conv(): lax.associative_scan(chain_step, (decays, loading), axis=1)  26.4 us
    unnamed x55, local copies, waits for them, and re-layouts  20.5 us
    slice x19, local copies, waits for them, and re-layouts, modal_conv(): lax.associative_scan(chain_step, (decays, loading), axis=1)  20.2 us
    gather x2, local copies, waits for them, and re-layouts, modal_conv(): toeplitz = jnp.where(offsets[None] >= 0, kernel[:, clipped], 0.0)  16.5 us
  transfers between devices with their start and end apart: 6, of which 5 were waited for; matrix products, arithmetic and copies ran while one was open for 22% of the time, Pallas kernels for 0%

commit v1 on v0

--- a/solution.py
+++ b/solution.py
@@ -6,6 +6,11 @@
 from jax.sharding import PartitionSpec as P
 
 highest = lax.Precision.HIGHEST
+
+
+def summed_here(x, mesh_axis):
+    terms = lax.all_gather(x, mesh_axis)
+    return jnp.sum(terms, axis=0)
 
 
 def from_behind(block, axis, distance):
@@ -85,7 +90,7 @@
     tok_rows, feature_width = activations.shape
     model_width = feature_width * lax.axis_size("mp")
     act_float = activations.astype(jnp.float32)
-    squares = lax.psum(jnp.sum(act_float * act_float, axis=1), "mp")
+    squares = summed_here(jnp.sum(act_float * act_float, axis=1), "mp")
     inverse = lax.rsqrt(squares / model_width + 1e-06)
     normed = (act_float * inverse[:, None] * norm_gain[None, :]).astype(jnp.bfloat16)
     panel = lax.all_gather(w_in, "ctx", axis=0, tiled=True).reshape(model_width, 3 * feature_width)

time: 459 us -> 483 us (1.052)
  waiting for transfers between devices: 205 us -> 228 us
  blocking collectives: 105 us -> 82.9 us
  local copies, waits for them, and re-layouts: 85.8 us -> 101 us
  other arithmetic: 17.2 us -> 24 us
    psum x1 -> x0, blocking collectives: 59.9 us -> none  [local(): squares = lax.psum(jnp.sum(act_float * act_float, axis=1), 'mp')]
    all_gather x0 -> x1, blocking collectives: none -> 37.7 us  [summed_here(): terms = lax.all_gather(x, mesh_axis)]
    all_gather x1, waiting for transfers between devices: 11.3 us -> 33.9 us  [local(): lax.all_gather(w_in, 'ctx', axis=0, tiled=True)]
    pad x12, local copies, waits for them, and re-layouts: 26.4 us -> 36.5 us  [modal_conv(): lax.associative_scan(chain_step, (decays, loading), axis=1)]
    unnamed x55 -> x43, local copies, waits for them, and re-layouts: 20.5 us -> 20.2 us
  transfers between devices with their start and end apart: 6 -> 6, of which waited for: 5 -> 5; matrix products, arithmetic and copies ran while one was open for 22% -> 26% of each run, Pallas kernels for 0% -> 0%
where the time goes in v1:
time: 483 us; the launch traced here: 481 us
  waiting for transfers between devices  228 us (47%)
  local copies, waits for them, and re-layouts  101 us (21%)
  blocking collectives  82.9 us (17%)
  other arithmetic  24 us (5%)
  matrix products  20.1 us (4%)
  between operations  14.4 us (3%)
  starting transfers between devices  10.7 us (2%)
    unnamed x5, waiting for transfers between devices  93.9 us
    all_gather x1, waiting for transfers between devices, local(): lax.all_gather(normed, 'mp', axis=1, tiled=True)  92.6 us
    all_gather x1, blocking collectives, summed_here(): terms = lax.all_gather(x, mesh_axis)  37.7 us
    pad x12, local copies, waits for them, and re-layouts, modal_conv(): lax.associative_scan(chain_step, (decays, loading), axis=1)  36.5 us
    all_gather x1, waiting for transfers between devices, local(): lax.all_gather(w_in, 'ctx', axis=0, tiled=True)  33.9 us
    all_gather x1, blocking collectives, local(): final_state = lax.all_gather(final_part, 'ctx', axis=0, tiled=True)  32.5 us
    slice x19, local copies, waits for them, and re-layouts, modal_conv(): lax.associative_scan(chain_step, (decays, loading), axis=1)  22.6 us
    unnamed x43, local copies, waits for them, and re-layouts  20.2 us
  transfers between devices with their start and end apart: 6, of which 5 were waited for; matrix products, arithmetic and copies ran while one was open for 26% of the time, Pallas kernels for 0%

profile of v1, /device:TPU:4, one launch (start us, length us, event | category | flops | bytes accessed | tf_op | source)
XLA Modules:
  0.0 480.9 jit_solution(4780699343409475472)
XLA Ops:
  10.5 37.7 %all-gather = f32[32768]{0:T(1024)S(1)} all-gather(f32[1024]{0:T(1024)S(1)} %fusion.2), channel_id=2, replica_groups=mesh['ctx'=8,'mp'=32] {'mp'}, dimensions={0}, use_global_device_ids=true | all-gather | bytes 135168 | tf_op jit(solution)/shard_map/all_gather | solution.py:12
  50.9 33.9 %all-gather.7.cloned.1.call-done = bf16[4096,3,128]{0,2,1:T(8,128)(2,1)} async-done(((bf16[512,3,128]{0,2,1:T(8,128)(2,1)}), bf16[4096,3,128]{0,2,1:T(8,128)(2,1)}) %all-gather.7.cloned.1.call-update) | async-done | bytes 3145744 | tf_op jit(solution)/shard_map/all_gather | solution.py:96
  84.8 92.6 %all-gather.5.cloned.1.call-done = bf16[1024,4096]{1,0:T(8,128)(2,1)} async-done(((bf16[1024,128]{1,0:T(8,128)(2,1)}), bf16[1024,4096]{1,0:T(8,128)(2,1)}) %all-gather.5.cloned.1.call-update) | async-done | bytes 8388624 | tf_op jit(solution)/shard_map/all_gather | solution.py:99
  177.4 7.7 %convolution_convert_fusion = bf16[1024,384]{0,1:T(8,128)(2,1)S(1)} fusion(bf16[1024,4096]{1,0:T(8,128)(2,1)} %all-gather.5.cloned.1.call-done, bf16[4096,384]{0,1:T(8,128)(2,1)} %bitcast.65), kind=kOutput, calls=%fused_computation.7 | convolution fusion | flops 3221618688 | bytes 12320768 | tf_op jit(solution)/shard_map/dot_general | solution.py:97
  185.2 4.0 collective-permute-start
  189.4 5.1 %collective-permute-done = bf16[3,128,2]{2,1,0:T(8,128)(2,1)S(1)} collective-permute-done((bf16[3,128,2]{2,1,0:T(8,128)(2,1)S(1)}, bf16[3,128,2]{2,1,0:T(8,128)(2,1)S(1)}, u32[]{:S(2)}, u32[]{:S(2)}) %collective-permute-start) | collective-permute-done | bytes 1568 | tf_op jit(solution)/shard_map/ppermute | solution.py:19
  197.0 6.7 %all-to-all-start = ((bf16[8,16,1024]{2,1,0:T(8,128)(2,1)}), bf16[8,16,1024]{2,1,0:T(8,128)(2,1)S(1)}, u32[]{:S(2)}, u32[]{:S(2)}) async-start(bf16[8,16,1024]{2,1,0:T(8,128)(2,1)} %bitcast.7), calls=%async_computation | async-start | bytes 524288 | tf_op jit(solution)/shard_map/all_to_all | solution.py:114
  211.5 2.9 slice.235
  214.4 2.3 slice.195
  216.7 2.3 slice.194
  239.8 6.2 %pad.47 = f32[16,4,16]{1,2,0:T(8,128)S(1)} pad(f32[16,2,16]{1,2,0:T(8,128)} %pad_add_fusion, f32[]{:T(128)} %constant.7.clone.1), padding=0_0_0x1_0_1x0_0_0 | pad | bytes 6148 | tf_op jit(solution)/shard_map/pad | solution.py:68
  247.7 6.2 %pad.46 = f32[16,4,16]{1,2,0:T(8,128)S(1)} pad(f32[16,2,16]{1,2,0:T(8,128)} %pad_maximum_fusion, f32[]{:T(128)} %constant.7.clone.1), padding=0_0_0x0_1_1x0_0_0 | pad | bytes 6148 | tf_op jit(solution)/shard_map/pad | solution.py:68
  256.9 6.3 %pad.49 = f32[16,8,16]{1,2,0:T(8,128)S(1)} pad(f32[16,4,16]{1,2,0:T(8,128)} %add.156, f32[]{:T(128)} %constant.7.clone.1), padding=0_0_0x1_0_1x0_0_0 | pad | bytes 12292 | tf_op jit(solution)/shard_map/pad | solution.py:68
  274.7 2.2 pad.55
  276.9 3.2 pad.95
  280.1 3.2 pad.57
  284.3 3.2 pad.56
  288.9 15.5 %gather_fusion = f32[4096,16]{1,0:T(8,128)} fusion(f32[16,64]{0,1:T(8,128)S(1)} %bitcast.53, s32[4096]{0:T(1024)} %broadcast_clamp_fusion), kind=kCustom, calls=%fused_computation | custom fusion | bytes 540672 | tf_op jit(solution)/shard_map/gather | solution.py:62
  304.3 2.3 copy.90
  314.8 12.7 %all_to_all.29 = f32[16,8,1024]{2,0,1:T(8,128)S(1)} all-to-all(f32[16,8,1024]{2,0,1:T(8,128)S(1)} %copy_add_fusion), channel_id=1, replica_groups=mesh['ctx'=8,'mp'=32] {'ctx'}, dimensions={1} | all-to-all | bytes 1048576 | tf_op jit(solution)/shard_map/all_to_all | solution.py:122
  327.7 6.9 %convert_bitcast_fusion = bf16[4096,1024]{0,1:T(8,128)(2,1)} fusion(bf16[128,1024]{1,0:T(8,128)(2,1)S(1)} %fusion.8, bf16[128,4096]{1,0:T(8,128)(2,1)} %all-gather.9.cloned.1.call-done), kind=kOutput, calls=%fused_computation.1 | convolution fusion | flops 1077936128 | bytes 9699328 | tf_op jit(solution)/shard_map/dot_general | solution.py:128
  334.6 11.6 %copy.103 = bf16[4096,1024]{1,0:T(8,128)(2,1)} copy(bf16[4096,1024]{0,1:T(8,128)(2,1)} %convert_bitcast_fusion) | data formatting | bytes 16777216
  346.2 32.5 %all_gather.23 = f32[128,16]{1,0:T(8,128)S(1)} all-gather(f32[16,16]{1,0:T(8,128)S(1)} %get-tuple-element.20), channel_id=1, replica_groups=mesh['ctx'=8,'mp'=32] {'ctx'}, dimensions={0}, use_global_device_ids=true | all-gather | bytes 9216 | tf_op jit(solution)/shard_map/all_gather | solution.py:123
  379.3 93.1 %reduce-scatter.4.cloned.1.call-done = bf16[128,1024]{1,0:T(8,128)(2,1)} async-done(((bf16[4096,1024]{1,0:T(8,128)(2,1)}), bf16[128,1024]{1,0:T(8,128)(2,1)}) %reduce-scatter.4.cloned.1.call-update) | async-done | bytes 262160
  (133 shorter events, 66.2 us)
Async XLA Ops:
  7.2 182.0 %copy-start = (f32[128,16]{0,1:T(8,128)S(1)}, f32[128,16]{0,1:T(8,128)}, u32[]{:S(2)}) copy-start(f32[128,16]{0,1:T(8,128)} %param.19) | copy-start | bytes 24580
  7.2 41.1 %copy-start.1 = (bf16[1024,128]{1,0:T(8,128)(2,1)S(1)}, bf16[1024,128]{1,0:T(8,128)(2,1)}, u32[]{:S(2)}) copy-start(bf16[1024,128]{1,0:T(8,128)(2,1)} %param.13) | copy-start | bytes 786436
  7.2 41.1 %copy-start.13 = (f32[128]{0:T(128)S(1)}, f32[128]{0:T(128)}, u32[]{:S(2)}) copy-start(f32[128]{0:T(128)} %param.14) | copy-start | bytes 1540
  7.2 42.8 %copy-start.11 = (f32[3,3,128]{2,1,0:T(4,128)S(1)}, f32[3,3,128]{2,1,0:T(4,128)}, u32[]{:S(2)}) copy-start(f32[3,3,128]{2,1,0:T(4,128)} %param.17) | copy-start | bytes 13828
  7.2 42.8 %copy-start.9 = (f32[128,16]{0,1:T(8,128)S(1)}, f32[128,16]{0,1:T(8,128)}, u32[]{:S(2)}) copy-start(f32[128,16]{0,1:T(8,128)} %param.21) | copy-start | bytes 24580
  7.2 42.8 %copy-start.10 = (f32[128,16]{0,1:T(8,128)S(1)}, f32[128,16]{0,1:T(8,128)}, u32[]{:S(2)}) copy-start(f32[128,16]{0,1:T(8,128)} %param.18) | copy-start | bytes 24580
  7.2 77.6 %all-gather.7.cloned.1.call-start = ((), (), s32[]{:S(2)}) async-start(), calls=%async_computation.4 | async-start | bytes 3538944 | tf_op jit(solution)/shard_map/all_gather | solution.py:96
  9.3 168.1 %all-gather.5.cloned.1.call-start = ((), (), s32[]{:S(2)}) async-start(), calls=%async_computation.3 | async-start | bytes 8650752 | tf_op jit(solution)/shard_map/all_gather | solution.py:99
  49.2 278.4 %all-gather.9.cloned.1.call-start = ((), (), s32[]{:S(2)}) async-start(), calls=%async_computation.5 | async-start | bytes 1179648 | tf_op jit(solution)/shard_map/all_gather | solution.py:125
  50.2 134.9 %copy-start.6 = (f32[16,16]{1,0:T(8,128)}, f32[16,16]{1,0:T(8,128)S(1)}, u32[]{:S(2)}) copy-start(f32[16,16]{1,0:T(8,128)S(1)} %copy.106) | copy-start | bytes 3076
  50.8 168.3 %copy-start.4 = (f32[16,16]{1,0:T(8,128)}, f32[16,16]{1,0:T(8,128)S(1)}, u32[]{:S(2)}) copy-start(f32[16,16]{1,0:T(8,128)S(1)} %get-tuple-element.27) | copy-start | bytes 3076
  50.8 172.8 %copy-start.5 = (f32[16,16]{1,0:T(8,128)}, f32[16,16]{1,0:T(8,128)S(1)}, u32[]{:S(2)}) copy-start(f32[16,16]{1,0:T(8,128)S(1)} %get-tuple-element.28) | copy-start | bytes 3076
  177.4 11.9 %copy-start.12 = (bf16[3,128,2]{1,2,0:T(2,128)(2,1)S(1)}, bf16[3,128,2]{1,2,0:T(2,128)(2,1)}, u32[]{:S(2)}) copy-start(bf16[3,128,2]{1,2,0:T(2,128)(2,1)} %param.16) | copy-start | bytes 4612
  185.2 9.4 %collective-permute-start = (bf16[3,128,2]{2,1,0:T(8,128)(2,1)S(1)}, bf16[3,128,2]{2,1,0:T(8,128)(2,1)S(1)}, u32[]{:S(2)}, u32[]{:S(2)}) collective-permute-start(bf16[3,128,2]{2,1,0:T(8,128)(2,1)S(1)} %slice.240), channel_id=1, source_target_pairs={{0,32},{32,64},{64,96},{96,128},{128,160},{160,192},{192,224},{1,3... | collective-permute-start | bytes 4616 | tf_op jit(solution)/shard_map/ppermute | solution.py:19
  196.2 8.0 %copy-start.16 = (f32[128]{0:T(128)S(1)}, f32[128]{0:T(128)}, u32[]{:S(2)}) copy-start(f32[128]{0:T(128)} %param.20) | copy-start | bytes 1540
  196.2 11.1 %copy-start.7 = (s32[4096]{0:T(1024)S(1)}, s32[4096]{0:T(1024)}, u32[]{:S(2)}) copy-start(s32[4096]{0:T(1024)} %constant.70) | copy-start | bytes 49156
  197.0 13.0 %all-to-all-start = ((bf16[8,16,1024]{2,1,0:T(8,128)(2,1)}), bf16[8,16,1024]{2,1,0:T(8,128)(2,1)S(1)}, u32[]{:S(2)}, u32[]{:S(2)}) async-start(bf16[8,16,1024]{2,1,0:T(8,128)(2,1)} %bitcast.7), calls=%async_computation | async-start | bytes 524288 | tf_op jit(solution)/shard_map/all_to_all | solution.py:114
  203.6 268.9 %reduce-scatter.4.cloned.1.call-start = ((), (), s32[]{:S(2)}) async-start(), calls=%async_computation.6 | async-start | bytes 8650752
  268.1 15.3 %copy-start.2 = (f32[16,63,16]{1,2,0:T(8,128)S(1)}, f32[16,63,16]{1,2,0:T(8,128)}, u32[]{:S(2)}) copy-start(f32[16,63,16]{1,2,0:T(8,128)} %slice.235) | copy-start | bytes 193540
  304.3 2.4 copy-start.8
  306.7 2.3 copy-start.3
  306.7 2.3 copy-start.15
  311.0 2.5 copy-start.14
Sparse Core Ops, SparseCore 0:
  10.5 74.2 all-gather.6
  87.2 90.1 all-gather.4
  179.9 49.9 all-gather.8
  346.3 126.1 reduce-scatter.3
